TPU v7x, 32 devices: a whole 2x2x4 slice. The times are simulated.
32 devices in a mesh: wide: 16 (over z, y, x), narrow: 2 (over core).
Axes of the slice: x: 2, y: 2, z: 4, core: 2. Of those that a mesh axis runs over, the one named last changes fastest.
Arguments:
- queries: bfloat16 [4096, 768], P(('wide', 'narrow')), may hold values from -40 to 40
- table: bfloat16 [2048, 768], P('wide'), may hold values from -6 to 6
- head: bfloat16 [768, 768], replicated, may hold values from -0.21875 to 0.21875
- pos_ids: int32 [4096], P(('wide', 'narrow')), may hold values from 0 to 2047, as said below
- neg_ids: int32 [4096, 8], P(('wide', 'narrow')), may hold values from 0 to 2047, as said below
- loss_weights: float32 [4096], P(('wide', 'narrow')), may hold values from 8 to 64
Outputs:
- d_queries: float32 [4096, 768], P(('wide', 'narrow'))
- d_table: float32 [2048, 768], P(('wide', 'narrow'))
- d_head: float32 [768, 768], replicated
Inputs may be any that keep to these rules, and one draw needn't show every extreme that they name: `pos_ids`: the queries form aligned blocks of 128 (the queries of one device). Within a block at most 16 positives lie in one shard of 128 consecutive passage rows (shard = id // 128); one shard, the same for every block, holds exactly 16 of every block. `neg_ids`: within each aligned block of 128 queries, at most 96 of its 1024 negatives lie in one shard of 128 consecutive passage rows (shard = id // 128); one shard, the same for every block, holds exactly 96 of every block. Popular rows recur.
All inputs are finite; a program needn't handle non-finite values.
Results may differ from a plain program's by a relative error of at most 0.0063.
Values may be sent and summed in bfloat16 or wider, within the bound.
A program may use at most 64 MiB of HBM per device.

v0:
```python
import jax
import jax.numpy as jnp
from jax import lax
from jax.sharding import PartitionSpec as P

BOTH = ("wide", "narrow")


def per_device(queries, table, head, pos_ids, neg_ids, loss_weights):
    wide_count = lax.axis_size("wide")
    narrow_count = lax.axis_size("narrow")
    width = queries.shape[1]
    shard_rows = table.shape[0]
    part_rows = shard_rows // narrow_count
    rows = shard_rows * wide_count
    scale = float(width) ** (-0.5)
    mine = lax.axis_index("narrow")
    my_table = lax.dynamic_slice_in_dim(table, mine * part_rows, part_rows, 0)
    my_proj = jnp.dot(my_table, head, preferred_element_type=jnp.float32).astype(jnp.bfloat16)
    table_proj = lax.all_gather(my_proj, BOTH, axis=0, tiled=True)
    group_pos = lax.all_gather(pos_ids, "narrow", axis=0, tiled=True)
    query_proj = jnp.dot(queries, head, preferred_element_type=jnp.float32).astype(jnp.bfloat16)
    columns = jnp.arange(rows, dtype=jnp.int32)
    key_count = jnp.sum((group_pos[:, None] == columns[None, :]).astype(jnp.float32), axis=0)
    own = (pos_ids[:, None] == columns[None, :]).astype(jnp.float32)
    count = jnp.broadcast_to(key_count[None, :], own.shape)
    for n in range(neg_ids.shape[1]):
        count = count + (neg_ids[:, n : n + 1] == columns[None, :]).astype(jnp.float32)
    scores = (
        lax.dot_general(
            query_proj, table_proj, (((1,), (1,)), ((), ())), preferred_element_type=jnp.float32
        )
        * scale
    )
    top = jnp.max(jnp.where(count > 0, scores, -jnp.inf), axis=1, keepdims=True)
    exps = jnp.where(count > 0, jnp.exp(jnp.minimum(scores - top, 0.0)), 0.0)
    total = jnp.sum(count * exps, axis=1, keepdims=True)
    probs = exps / total
    weight = loss_weights[:, None] * scale
    coef = (weight * probs).astype(jnp.bfloat16).astype(jnp.float32)
    own_coef = (weight * (probs - 1.0)).astype(jnp.bfloat16).astype(jnp.float32)
    coef = ((count - own) * coef + own * own_coef).astype(jnp.bfloat16)
    grad_query = jnp.dot(coef, table_proj, preferred_element_type=jnp.float32).astype(jnp.bfloat16)
    d_queries = lax.dot_general(
        grad_query, head, (((1,), (1,)), ((), ())), preferred_element_type=jnp.float32
    )
    row_partial = lax.dot_general(
        coef, query_proj, (((0,), (0,)), ((), ())), preferred_element_type=jnp.float32
    ).astype(jnp.bfloat16)
    pieces = lax.all_to_all(row_partial, BOTH, split_axis=0, concat_axis=0, tiled=True)
    row_grad = jnp.sum(pieces.reshape(-1, part_rows, width).astype(jnp.float32), axis=0)
    row_grad = row_grad.astype(jnp.bfloat16)
    d_table = lax.dot_general(
        row_grad, head, (((1,), (1,)), ((), ())), preferred_element_type=jnp.float32
    )
    head_part = lax.dot_general(
        queries, grad_query, (((0,), (0,)), ((), ())), preferred_element_type=jnp.float32
    )
    head_part = head_part + lax.dot_general(
        my_table, row_grad, (((0,), (0,)), ((), ())), preferred_element_type=jnp.float32
    )
    d_head = lax.psum(head_part, BOTH)
    return (d_queries, d_table, d_head)


def solution(mesh):
    placed = (P(BOTH, None), P("wide", None), P(), P(BOTH), P(BOTH, None), P(BOTH))
    return jax.shard_map(
        per_device,
        mesh=mesh,
        in_specs=placed,
        out_specs=(P(BOTH, None), P(BOTH, None), P()),
        check_vma=False,
    )
```

profile of v0, /device:TPU:0, one launch (start us, length us, event | category | flops | bytes accessed | tf_op | source)
XLA Modules:
  0.0 308.6 jit_solution(17481606412836012648)
XLA Ops:
  7.2 0.0 copy-start
  7.2 0.0 all-gather.3.cloned.1.call-start
  7.2 1.2 copy-done
  8.4 1.9 convolution_convert_fusion.3
  10.3 0.0 all-gather.3.cloned.1.call-update
  10.3 2.1 all-gather
  12.4 0.3 convert_reduce_fusion
  12.8 0.7 broadcast_multiply_fusion
  13.4 1.0 slice_bitcast_fusion.7
  14.4 1.2 convolution_convert_fusion.2
  15.7 57.6 %all-gather.3.cloned.1.call-done = bf16[2048,768]{1,0:T(8,128)(2,1)} async-done(((bf16[64,768]{1,0:T(8,128)(2,1)}), bf16[2048,768]{1,0:T(8,128)(2,1)}) %all-gather.3.cloned.1.call-update) | async-done | bytes 3145744 | tf_op jit(solution)/shard_map/all_gather | solution.py:20
  73.3 3.7 %select_reduce_fusion = (f32[128]{0:T(128)S(1)}, f32[128,2048]{1,0:T(8,128)S(1)}) fusion(s32[128]{0:T(128)S(1)} %get-tuple-element.18, s32[128]{0:T(128)S(1)} %get-tuple-element.19, s32[128]{0:T(128)S(1)} %get-tuple-element.13, s32[128]{0:T(128)S(1)} %get-tuple-element.14, s32[128]{0:T(128)S(1)} %get-tuple-element.15, s32[128]{0:T(128)S(1)} %get-tuple-element.16, ...), kind=kOutput, calls=%fused_computation.13 | convolution fusion | flops 409993088 | bytes 4403712 | tf_op jit(solution)/shard_map/dot_general | solution.py:30
  77.0 1.5 multiply_reduce_fusion
  78.5 0.0 copy-done.5
  78.5 4.2 %convolution_convert_fusion = bf16[2048,768]{1,0:T(8,128)(2,1)} fusion(bf16[128,768]{1,0:T(8,128)(2,1)S(1)} %convolution_convert_fusion.2, f32[128,2048]{1,0:T(8,128)S(1)} %get-tuple-element.21, f32[128]{0:T(128)S(1)} %multiply_reduce_fusion, f32[128]{0:T(128)S(1)} %get-tuple-element.20, f32[128]{0:T(128)S(1)} %broadcast_multiply_fusion, ...), kind=kOutput, calls=%fused_computation | convolution fusion | flops 415498240 | bytes 4405248 | tf_op jit(solution)/shard_map/dot_general | solution.py:47
  82.8 3.5 %all-to-all-start = ((bf16[32,64,768]{2,1,0:T(8,128)(2,1)}), bf16[32,64,768]{2,1,0:T(8,128)(2,1)}, u32[]{:S(2)}, u32[]{:S(2)}) async-start(bf16[32,64,768]{2,1,0:T(8,128)(2,1)} %bitcast.35), calls=%async_computation | async-start | bytes 6291456 | tf_op jit(solution)/shard_map/all_to_all | solution.py:50
  86.3 0.0 all-reduce.2.cloned.1.call-start
  86.3 0.0 copy-start.2
  86.3 4.1 %convolution_convert_fusion.1 = bf16[128,768]{1,0:T(8,128)(2,1)S(1)} fusion(bf16[2048,768]{1,0:T(8,128)(2,1)} %all-gather.3.cloned.1.call-done, f32[128,2048]{1,0:T(8,128)S(1)} %get-tuple-element.21, f32[128]{0:T(128)S(1)} %multiply_reduce_fusion, f32[128]{0:T(128)S(1)} %get-tuple-element.20, f32[128]{0:T(128)S(1)} %broadcast_multiply_fusion, ...), kind=kOutput, calls=%fused_computation.5 | convolution fusion | flops 414023680 | bytes 4405248 | tf_op jit(solution)/shard_map/dot_general | solution.py:43
  90.4 0.0 copy-start.3
  90.4 0.7 copy-done.3
  91.1 0.0 copy-done.2
  91.1 0.5 fusion.7
  91.6 66.1 %all-to-all-done = bf16[32,64,768]{2,1,0:T(8,128)(2,1)} async-done(((bf16[32,64,768]{2,1,0:T(8,128)(2,1)}), bf16[32,64,768]{2,1,0:T(8,128)(2,1)}, u32[]{:S(2)}, u32[]{:S(2)}) %all-to-all-start) | async-done | bytes 3145760 | tf_op jit(solution)/shard_map/all_to_all | solution.py:50
  157.7 3.0 reduce_sum.32
  160.7 2.9 bitcast_add_fusion
  163.5 0.0 all-reduce.2.cloned.1.call-update
  163.5 0.9 copy-done.4
  164.4 1.3 fusion.5
  165.7 1.2 fusion.6
  166.9 131.8 %all-reduce.2.cloned.1.call-done = f32[768,768]{0,1:T(8,128)} async-done(((f32[768,768]{0,1:T(8,128)}), f32[768,768]{0,1:T(8,128)}) %all-reduce.2.cloned.1.call-update) | async-done | bytes 2359312 | tf_op jit(solution)/shard_map/psum | solution.py:62
  298.7 3.0 copy.14
  (4 shorter events, 0.0 us)
Async XLA Ops:
  7.2 1.3 copy-start
  7.2 66.1 %all-gather.3.cloned.1.call-start = ((), (), s32[]{:S(2)}) async-start(), calls=%async_computation.1 | async-start | bytes 3244032 | tf_op jit(solution)/shard_map/all_gather | solution.py:20
  73.3 5.2 %copy-start.5 = (s32[128]{0:T(128)S(1)}, s32[128]{0:T(128)}, u32[]{:S(2)}) copy-start(s32[128]{0:T(128)} %param.9) | copy-start | bytes 1540
  82.8 74.9 %all-to-all-start = ((bf16[32,64,768]{2,1,0:T(8,128)(2,1)}), bf16[32,64,768]{2,1,0:T(8,128)(2,1)}, u32[]{:S(2)}, u32[]{:S(2)}) async-start(bf16[32,64,768]{2,1,0:T(8,128)(2,1)} %bitcast.35), calls=%async_computation | async-start | bytes 6291456 | tf_op jit(solution)/shard_map/all_to_all | solution.py:50
  86.3 212.4 %all-reduce.2.cloned.1.call-start = ((), (), s32[]{:S(2)}) async-start(), calls=%async_computation.2 | async-start | bytes 4718592 | tf_op jit(solution)/shard_map/psum | solution.py:62
  86.3 4.8 %copy-start.2 = (bf16[128,768]{1,0:T(8,128)(2,1)S(1)}, bf16[128,768]{1,0:T(8,128)(2,1)}, u32[]{:S(2)}) copy-start(bf16[128,768]{1,0:T(8,128)(2,1)} %param.6) | copy-start | bytes 589828
  90.4 0.7 copy-start.3
  163.5 0.9 copy-start.4
  163.5 2.2 copy-start.1
Sparse Core Ops, SparseCore 0:
  11.4 61.7 all-gather.2
  163.7 135.0 all-reduce.1
where the time goes:
time: 309 us
  waiting for transfers between devices  256 us (83%)
  matrix products  20.9 us (7%)
  between operations  14.1 us (5%)
  local copies, waits for them, and re-layouts  6.83 us (2%)
  other arithmetic  5.46 us (2%)
  starting transfers between devices  3.6 us (1%)
    psum x1, waiting for transfers between devices, per_device(): d_head = lax.psum(head_part, BOTH)  132 us
    all_to_all x1, waiting for transfers between devices, per_device(): lax.all_to_all(row_partial, BOTH, split_axis=0, concat_axis=0, tiled=True)  66.1 us
    all_gather x1, waiting for transfers between devices, per_device(): table_proj = lax.all_gather(my_proj, BOTH, axis=0, tiled=True)  57.6 us
  transfers between devices with their start and end apart: 3, of which 3 were waited for; matrix products, arithmetic and copies ran while one was open for 3% of the time, Pallas kernels for 0%

commit v1 on v0

--- a/solution.py
+++ b/solution.py
@@ -59,7 +59,7 @@
     head_part = head_part + lax.dot_general(
         my_table, row_grad, (((0,), (0,)), ((), ())), preferred_element_type=jnp.float32
     )
-    d_head = lax.psum(head_part, BOTH)
+    d_head = lax.psum(lax.psum(head_part, "narrow"), "wide")
     return (d_queries, d_table, d_head)
 
 

time: 309 us -> 333 us (1.078)
  waiting for transfers between devices: 256 us -> 281 us
    psum x1 -> x2, waiting for transfers between devices: 132 us -> 157 us  [per_device(): d_head = lax.psum(lax.psum(head_part, 'narrow'), 'wide')]
  transfers between devices with their start and end apart: 3 -> 4, of which waited for: 3 -> 4; matrix products, arithmetic and copies ran while one was open for 3% -> 3% of each run, Pallas kernels for 0% -> 0%
where the time goes in v1:
time: 333 us
  waiting for transfers between devices  281 us (84%)
  matrix products  21 us (6%)
  between operations  13.8 us (4%)
  local copies, waits for them, and re-layouts  5.93 us (2%)
  other arithmetic  5.47 us (2%)
  starting transfers between devices  3.65 us (1%)
    psum x2, waiting for transfers between devices, per_device(): d_head = lax.psum(lax.psum(head_part, 'narrow'), 'wide')  157 us
    all_to_all x1, waiting for transfers between devices, per_device(): lax.all_to_all(row_partial, BOTH, split_axis=0, concat_axis=0, tiled=True)  66.1 us
    all_gather x1, waiting for transfers between devices, per_device(): table_proj = lax.all_gather(my_proj, BOTH, axis=0, tiled=True)  57.6 us
  transfers between devices with their start and end apart: 4, of which 4 were waited for; matrix products, arithmetic and copies ran while one was open for 3% of the time, Pallas kernels for 0%

profile of v1, /device:TPU:0, one launch (start us, length us, event | category | flops | bytes accessed | tf_op | source)
XLA Modules:
  0.0 332.7 jit_solution(11036797139654866939)
XLA Ops:
  7.2 0.0 copy-start
  7.2 0.0 all-gather.3.cloned.1.call-start
  7.2 1.2 copy-done
  8.4 1.9 convolution_convert_fusion.3
  10.3 0.0 all-gather.3.cloned.1.call-update
  10.3 2.1 all-gather
  12.4 0.3 convert_reduce_fusion
  12.8 0.7 broadcast_multiply_fusion
  13.4 1.0 slice_bitcast_fusion.7
  14.4 1.2 convolution_convert_fusion.2
  15.7 57.6 %all-gather.3.cloned.1.call-done = bf16[2048,768]{1,0:T(8,128)(2,1)} async-done(((bf16[64,768]{1,0:T(8,128)(2,1)}), bf16[2048,768]{1,0:T(8,128)(2,1)}) %all-gather.3.cloned.1.call-update) | async-done | bytes 3145744 | tf_op jit(solution)/shard_map/all_gather | solution.py:20
  73.3 3.7 %select_reduce_fusion = (f32[128]{0:T(128)S(1)}, f32[128,2048]{1,0:T(8,128)S(1)}) fusion(s32[128]{0:T(128)S(1)} %get-tuple-element.18, s32[128]{0:T(128)S(1)} %get-tuple-element.19, s32[128]{0:T(128)S(1)} %get-tuple-element.13, s32[128]{0:T(128)S(1)} %get-tuple-element.14, s32[128]{0:T(128)S(1)} %get-tuple-element.15, s32[128]{0:T(128)S(1)} %get-tuple-element.16, ...), kind=kOutput, calls=%fused_computation.13 | convolution fusion | flops 409993088 | bytes 4403712 | tf_op jit(solution)/shard_map/dot_general | solution.py:30
  77.0 1.5 multiply_reduce_fusion
  78.5 4.2 %convolution_convert_fusion = bf16[2048,768]{1,0:T(8,128)(2,1)} fusion(bf16[128,768]{1,0:T(8,128)(2,1)S(1)} %convolution_convert_fusion.2, f32[128,2048]{1,0:T(8,128)S(1)} %get-tuple-element.21, f32[128]{0:T(128)S(1)} %multiply_reduce_fusion, f32[128]{0:T(128)S(1)} %get-tuple-element.20, f32[128]{0:T(128)S(1)} %broadcast_multiply_fusion, ...), kind=kOutput, calls=%fused_computation | convolution fusion | flops 415498240 | bytes 4405248 | tf_op jit(solution)/shard_map/dot_general | solution.py:47
  82.8 3.5 %all-to-all-start = ((bf16[32,64,768]{2,1,0:T(8,128)(2,1)}), bf16[32,64,768]{2,1,0:T(8,128)(2,1)}, u32[]{:S(2)}, u32[]{:S(2)}) async-start(bf16[32,64,768]{2,1,0:T(8,128)(2,1)} %bitcast.35), calls=%async_computation | async-start | bytes 6291456 | tf_op jit(solution)/shard_map/all_to_all | solution.py:50
  86.3 0.0 all-reduce.3.cloned.1.call-start
  86.3 0.0 copy-start.2
  86.3 4.1 %convolution_convert_fusion.1 = bf16[128,768]{1,0:T(8,128)(2,1)S(1)} fusion(bf16[2048,768]{1,0:T(8,128)(2,1)} %all-gather.3.cloned.1.call-done, f32[128,2048]{1,0:T(8,128)S(1)} %get-tuple-element.21, f32[128]{0:T(128)S(1)} %multiply_reduce_fusion, f32[128]{0:T(128)S(1)} %get-tuple-element.20, f32[128]{0:T(128)S(1)} %broadcast_multiply_fusion, ...), kind=kOutput, calls=%fused_computation.5 | convolution fusion | flops 414023680 | bytes 4405248 | tf_op jit(solution)/shard_map/dot_general | solution.py:43
  90.4 0.0 copy-start.3
  90.4 0.7 copy-done.3
  91.1 0.5 fusion.7
  91.6 66.1 %all-to-all-done = bf16[32,64,768]{2,1,0:T(8,128)(2,1)} async-done(((bf16[32,64,768]{2,1,0:T(8,128)(2,1)}), bf16[32,64,768]{2,1,0:T(8,128)(2,1)}, u32[]{:S(2)}, u32[]{:S(2)}) %all-to-all-start) | async-done | bytes 3145760 | tf_op jit(solution)/shard_map/all_to_all | solution.py:50
  157.7 3.0 reduce_sum.32
  160.7 2.9 bitcast_add_fusion
  163.5 0.0 all-reduce.3.cloned.1.call-update
  163.5 0.0 all-reduce.5.cloned.1.call-start
  163.6 21.2 %all-reduce.3.cloned.1.call-done = f32[768,768]{0,1:T(8,128)} async-done(((f32[768,768]{0,1:T(8,128)}), f32[768,768]{0,1:T(8,128)}) %all-reduce.3.cloned.1.call-update) | async-done | bytes 2359312 | tf_op jit(solution)/shard_map/psum | solution.py:62
  184.8 0.0 all-reduce.5.cloned.1.call-update
  184.8 1.3 fusion.5
  186.1 1.2 fusion.6
  187.3 135.8 %all-reduce.5.cloned.1.call-done = f32[768,768]{0,1:T(8,128)} async-done(((f32[768,768]{0,1:T(8,128)}), f32[768,768]{0,1:T(8,128)}) %all-reduce.5.cloned.1.call-update) | async-done | bytes 2359312 | tf_op jit(solution)/shard_map/psum | solution.py:62
  323.1 3.0 copy.14
  (7 shorter events, 0.0 us)
Async XLA Ops:
  7.2 1.3 copy-start
  7.2 66.1 %all-gather.3.cloned.1.call-start = ((), (), s32[]{:S(2)}) async-start(), calls=%async_computation.1 | async-start | bytes 3244032 | tf_op jit(solution)/shard_map/all_gather | solution.py:20
  73.3 5.2 %copy-start.5 = (s32[128]{0:T(128)S(1)}, s32[128]{0:T(128)}, u32[]{:S(2)}) copy-start(s32[128]{0:T(128)} %param.9) | copy-start | bytes 1540
  82.8 74.9 %all-to-all-start = ((bf16[32,64,768]{2,1,0:T(8,128)(2,1)}), bf16[32,64,768]{2,1,0:T(8,128)(2,1)}, u32[]{:S(2)}, u32[]{:S(2)}) async-start(bf16[32,64,768]{2,1,0:T(8,128)(2,1)} %bitcast.35), calls=%async_computation | async-start | bytes 6291456 | tf_op jit(solution)/shard_map/all_to_all | solution.py:50
  86.3 98.5 %all-reduce.3.cloned.1.call-start = ((), (), s32[]{:S(2)}) async-start(), calls=%async_computation.2 | async-start | bytes 4718592 | tf_op jit(solution)/shard_map/psum | solution.py:62
  86.3 4.8 %copy-start.2 = (bf16[128,768]{1,0:T(8,128)(2,1)S(1)}, bf16[128,768]{1,0:T(8,128)(2,1)}, u32[]{:S(2)}) copy-start(bf16[128,768]{1,0:T(8,128)(2,1)} %param.6) | copy-start | bytes 589828
  90.4 0.7 copy-start.3
  163.5 21.3 %copy-start.4 = (bf16[128,768]{1,0:T(8,128)(2,1)S(1)}, bf16[128,768]{1,0:T(8,128)(2,1)}, u32[]{:S(2)}) copy-start(bf16[128,768]{1,0:T(8,128)(2,1)} %copy-done.3) | copy-start | bytes 589828
  163.5 22.6 %copy-start.1 = (bf16[64,768]{1,0:T(8,128)(2,1)S(1)}, bf16[64,768]{1,0:T(8,128)(2,1)}, u32[]{:S(2)}) copy-start(bf16[64,768]{1,0:T(8,128)(2,1)} %reduce_sum.32) | copy-start | bytes 294916
  163.5 159.6 %all-reduce.5.cloned.1.call-start = ((), (), s32[]{:S(2)}) async-start(), calls=%async_computation.3 | async-start | bytes 4718592 | tf_op jit(solution)/shard_map/psum | solution.py:62
Sparse Core Ops, SparseCore 0:
  11.4 61.7 all-gather.2
  163.7 21.0 all-reduce.2
  190.4 132.6 all-reduce.4
